TPU v7x, 1024 devices: a whole 8x8x8 slice. The times are simulated.
1024 devices in a mesh: lane: 32 (over y, x_lo), section: 2 (over core), tp: 16 (over z, x_hi).
Axes of the slice: x: 8 (x_hi: 2, x_lo: 4; x = x_hi * 4 + x_lo), y: 8, z: 8, core: 2. Of those that a mesh axis runs over, the one named last changes fastest.
Arguments:
- merge_hidden: bfloat16 [16384, 5120], P('lane', 'section'), may hold values from -6 to 6
- merge_weight: bfloat16 [5120, 8192], P('section', 'tp'), may hold values from -0.25 to 0.25
- merge_bias: float32 [8192], P('tp'), may hold values from -3 to 3
- row_dest: int32 [16384], P(('lane', 'section')), may hold values from -1 to 31, as said below
- image_pos: int32 [32, 2, 32, 4], P('lane', 'section'), may hold values from -1 to 255, as said below
- text_embed: bfloat16 [16384, 8192], P(('lane', 'section'), 'tp'), may hold values from -8 to 8
- norm_gain: float32 [8192], P('tp'), may hold values from 0.25 to 1.75
- kv_weight: bfloat16 [8192, 2048], P('tp'), may hold values from -0.0625 to 0.0625
- kv_grad: bfloat16 [16384, 2048], P(('lane', 'section')), may hold values from -6 to 6
Outputs:
- key_value: bfloat16 [16384, 2048], P(('lane', 'section'), 'tp')
- embed_grad: bfloat16 [16384, 8192], P(('lane', 'section'), 'tp')
- image_grad: bfloat16 [16384, 8192], P(('lane', 'section'), 'tp')
Inputs may be any that keep to these rules, and one draw needn't show every extreme that they name: `row_dest`: rows come in blocks of 256: block s of lane j is rows j * 512 + s * 256 onward. Rows of one block that go to one lane number at most 4; every block sends 4 rows to some lane, and for every s some lane receives 4 rows from block s of every lane. image_pos[l, s, j, k] is the position, among the 256 tokens of block s of lane l (tokens l * 512 + s * 256 onward), of the k-th row (in row order) that block s of lane j sends to lane l, and -1 where that block sends fewer than k + 1 rows to lane l; the positions taken in one block are distinct.
All inputs are finite; a program needn't handle non-finite values.
Results may differ from a plain program's by a relative error of at most 0.007.
Values may be sent and summed in bfloat16 or wider, within the bound.
A program may use at most 32 MiB of HBM per device.

v0:
```python
import jax
import jax.numpy as jnp
from jax import lax
from jax.sharding import PartitionSpec as P

D = 8192


EPSILON = 1e-06


def on_device(
    merge_hidden,
    merge_weight,
    merge_bias,
    row_dest,
    image_pos,
    text_embed,
    norm_gain,
    kv_weight,
    kv_grad,
):
    lane_count = lax.axis_size("lane")
    tp_count = lax.axis_size("tp")
    slot_count = image_pos.shape[3]
    tokens = text_embed.shape[0]
    activated = jax.nn.gelu(merge_hidden.astype(jnp.float32), approximate=False).astype(
        jnp.bfloat16
    )
    merged = lax.psum_scatter(
        jnp.dot(activated, merge_weight, preferred_element_type=jnp.float32).astype(jnp.bfloat16),
        "section",
        scatter_dimension=0,
        tiled=True,
    ).astype(jnp.float32)
    image_block = (merged + merge_bias).astype(jnp.bfloat16)
    lane_ids = jnp.arange(lane_count, dtype=jnp.int32)
    matches = (row_dest[:, None] == lane_ids[None, :]).astype(jnp.int32)
    before = jnp.cumsum(matches, axis=0) - matches
    row_rank = jnp.sum(before * matches, axis=1)
    slot_ids = jnp.where(row_dest >= 0, row_dest * slot_count + row_rank, -1)
    send_table = (
        slot_ids[:, None] == jnp.arange(lane_count * slot_count, dtype=jnp.int32)[None, :]
    ).astype(jnp.bfloat16)
    outgoing = jnp.dot(send_table.T, image_block, preferred_element_type=jnp.float32).astype(
        jnp.bfloat16
    )
    arrived = lax.all_to_all(
        outgoing.reshape(lane_count, slot_count, -1),
        "lane",
        split_axis=0,
        concat_axis=0,
        tiled=True,
    )
    positions = image_pos.reshape(-1)
    place_match = positions[None, :] == jnp.arange(tokens, dtype=jnp.int32)[:, None]
    is_image = jnp.any(place_match, axis=1)
    place_table = place_match.astype(jnp.bfloat16)
    image_part = jnp.dot(
        place_table,
        arrived.reshape(lane_count * slot_count, -1),
        preferred_element_type=jnp.float32,
    ).astype(jnp.bfloat16)
    stream = jnp.where(is_image[:, None], image_part, text_embed)
    widened = stream.astype(jnp.float32)
    squares = jnp.sum(widened * widened, axis=1)
    normed_grad = lax.dot_general(
        kv_grad, kv_weight, (((1,), (1,)), ((), ())), preferred_element_type=jnp.float32
    )
    dot_terms = jnp.sum(widened * norm_gain * normed_grad, axis=1)
    total_squares, total_dots = lax.psum((squares, dot_terms), "tp")
    inv_rms = lax.rsqrt(total_squares / D + EPSILON)[:, None]
    normed = (widened * inv_rms * norm_gain).astype(jnp.bfloat16)
    col_size = kv_weight.shape[1] // tp_count
    product = jnp.dot(normed, kv_weight, preferred_element_type=jnp.float32)
    kv_block = lax.psum_scatter(
        jnp.transpose(product.reshape(tokens, 1 * lax.axis_size("tp"), col_size), (1, 0, 2)),
        "tp",
        scatter_dimension=0,
        tiled=True,
    )[0]
    key_value = kv_block.astype(jnp.bfloat16)
    embed_wide = inv_rms * norm_gain * normed_grad - widened * inv_rms**3 * total_dots[:, None] / D
    embed_grad = embed_wide.astype(jnp.bfloat16)
    returning = jnp.dot(place_table.T, embed_grad, preferred_element_type=jnp.float32).astype(
        jnp.bfloat16
    )
    returned = lax.all_to_all(
        returning.reshape(lane_count, slot_count, -1),
        "lane",
        split_axis=0,
        concat_axis=0,
        tiled=True,
    )
    image_grad = jnp.dot(
        send_table,
        returned.reshape(lane_count * slot_count, -1),
        preferred_element_type=jnp.float32,
    ).astype(jnp.bfloat16)
    return (key_value, embed_grad, image_grad)


def solution(mesh):
    in_specs = (
        P("lane", "section"),
        P("section", "tp"),
        P("tp"),
        P(("lane", "section")),
        P("lane", "section", None, None),
        P(("lane", "section"), "tp"),
        P("tp"),
        P("tp", None),
        P(("lane", "section"), None),
    )
    out_specs = (
        P(("lane", "section"), "tp"),
        P(("lane", "section"), "tp"),
        P(("lane", "section"), "tp"),
    )
    return jax.shard_map(
        on_device, mesh=mesh, in_specs=in_specs, out_specs=out_specs, check_vma=False
    )
```

profile of v0, /device:TPU:16, one launch (start us, length us, event | category | flops | bytes accessed | tf_op | source)
XLA Modules:
  0.0 370.6 jit_solution(12649081696183955475)
XLA Ops:
  7.3 1.6 copy-done
  8.9 13.5 %fusion.33 = bf16[512,512]{1,0:T(8,128)(2,1)} fusion(bf16[2560,512]{1,0:T(8,128)(2,1)S(1)} %copy-done, bf16[512,2560]{1,0:T(8,128)(2,1)} %param.9), kind=kOutput, calls=%fused_computation.37 | convolution fusion | flops 1428946944 | bytes 5767168 | tf_op jit(solution)/shard_map/dot_general | solution.py:31
  22.5 0.6 reduce-window.6
  23.1 0.2 slice_reduce_fusion
  23.3 0.1 fusion.48
  23.4 29.0 %reduce-scatter.3.cloned.1.call-done = bf16[256,512]{1,0:T(8,128)(2,1)} async-done(((bf16[512,512]{1,0:T(8,128)(2,1)}), bf16[256,512]{1,0:T(8,128)(2,1)}) %reduce-scatter.3.cloned.1.call-update) | async-done | bytes 262160 | tf_op jit(solution)/shard_map/reduce_scatter | solution.py:30
  52.4 1.2 convolution_convert_fusion.3
  53.7 0.7 reshape.49
  54.4 10.2 %all-to-all-start = ((bf16[32,4,512]{2,1,0:T(4,128)(2,1)}), bf16[32,4,512]{2,1,0:T(4,128)(2,1)S(1)}, u32[]{:S(2)}, u32[]{:S(2)}) async-start(bf16[32,4,512]{2,1,0:T(4,128)(2,1)} %reshape.49), calls=%async_computation.1 | async-start | bytes 262144 | tf_op jit(solution)/shard_map/all_to_all | solution.py:48
  64.6 0.1 copy.17
  64.7 0.1 eq.51
  64.8 0.1 fusion.41
  65.0 9.5 %all-to-all-done = bf16[32,4,512]{2,1,0:T(4,128)(2,1)S(1)} async-done(((bf16[32,4,512]{2,1,0:T(4,128)(2,1)}), bf16[32,4,512]{2,1,0:T(4,128)(2,1)S(1)}, u32[]{:S(2)}, u32[]{:S(2)}) %all-to-all-start) | async-done | bytes 131104 | tf_op jit(solution)/shard_map/all_to_all | solution.py:48
  74.5 0.2 fusion.37
  74.8 3.5 multiply_reduce_fusion
  78.2 53.9 %all-reduce = (f32[256]{0:T(256)S(1)}, f32[256]{0:T(256)S(1)}) all-reduce(f32[256]{0:T(256)S(1)} %get-tuple-element.4, f32[256]{0:T(256)S(1)} %get-tuple-element.3), channel_id=1, replica_groups=mesh['lane'=32,'section'=2,'tp'=16] {'tp'}, use_global_device_ids=true, to_apply=%region_6.7 | all-reduce | flops 512 | bytes 4096 | tf_op jit(solution)/shard_map/psum | solution.py:71
  132.1 2.3 convolution_bitcast_fusion
  134.5 1.6 copy.24
  136.0 1.2 subtract_convert_fusion
  137.3 0.2 convolution_convert_fusion.2
  137.6 14.0 %all_to_all.10 = bf16[32,4,512]{2,1,0:T(4,128)(2,1)S(1)} all-to-all(bf16[32,4,512]{2,1,0:T(4,128)(2,1)S(1)} %reshape.52), channel_id=1, replica_groups=mesh['lane'=32,'section'=2,'tp'=16] {'lane'}, dimensions={0} | all-to-all | bytes 262144 | tf_op jit(solution)/shard_map/all_to_all | solution.py:88
  151.6 1.0 convolution_convert_fusion
  152.6 209.7 %reduce-scatter.5.cloned.1.call-done = f32[1,256,128]{2,1,0:T(8,128)} async-done(((f32[16,256,128]{2,1,0:T(8,128)}), f32[1,256,128]{2,1,0:T(8,128)}) %reduce-scatter.5.cloned.1.call-update) | async-done | bytes 131088 | tf_op jit(solution)/shard_map/reduce_scatter | solution.py:76
  362.2 1.5 convert_bitcast_fusion
  (25 shorter events, 0.3 us)
Async XLA Ops:
  7.2 1.7 copy-start
  7.2 15.3 %copy-start.4 = (s32[256]{0:T(256)S(1)}, s32[256]{0:T(256)}, u32[]{:S(2)}) copy-start(s32[256]{0:T(256)} %param.12) | copy-start | bytes 3076
  7.2 45.2 %copy-start.5 = (f32[512]{0:T(512)S(1)}, f32[512]{0:T(512)}, u32[]{:S(2)}) copy-start(f32[512]{0:T(512)} %param.11) | copy-start | bytes 6148
  7.2 57.4 %copy-start.6 = (s32[1,1,32,4]{2,3,1,0:T(4,128)S(1)}, s32[1,1,32,4]{2,3,1,0:T(4,128)}, u32[]{:S(2)}) copy-start(s32[1,1,32,4]{2,3,1,0:T(4,128)} %param.13) | copy-start | bytes 1540
  7.2 67.3 %copy-start.2 = (bf16[256,512]{1,0:T(8,128)(2,1)S(1)}, bf16[256,512]{1,0:T(8,128)(2,1)}, u32[]{:S(2)}) copy-start(bf16[256,512]{1,0:T(8,128)(2,1)} %param.14) | copy-start | bytes 786436
  7.2 45.2 %reduce-scatter.3.cloned.1.call-start = ((), (), s32[]{:S(2)}) async-start(), calls=%async_computation.4 | async-start | bytes 786432 | tf_op jit(solution)/shard_map/reduce_scatter | solution.py:30
  22.5 52.3 %copy-start.3 = (f32[512]{0:T(512)S(1)}, f32[512]{0:T(512)}, u32[]{:S(2)}) copy-start(f32[512]{0:T(512)} %param.15) | copy-start | bytes 6148
  54.4 20.1 %all-to-all-start = ((bf16[32,4,512]{2,1,0:T(4,128)(2,1)}), bf16[32,4,512]{2,1,0:T(4,128)(2,1)S(1)}, u32[]{:S(2)}, u32[]{:S(2)}) async-start(bf16[32,4,512]{2,1,0:T(4,128)(2,1)} %reshape.49), calls=%async_computation.1 | async-start | bytes 262144 | tf_op jit(solution)/shard_map/all_to_all | solution.py:48
  64.6 297.6 %reduce-scatter.5.cloned.1.call-start = ((), (), s32[]{:S(2)}) async-start(), calls=%async_computation.5 | async-start | bytes 2228224 | tf_op jit(solution)/shard_map/reduce_scatter | solution.py:76
  137.3 226.5 %copy-start.1 = (bf16[256,512]{1,0:T(8,128)(2,1)}, bf16[256,512]{1,0:T(8,128)(2,1)S(1)}, u32[]{:S(2)}) copy-start(bf16[256,512]{1,0:T(8,128)(2,1)S(1)} %subtract_convert_fusion) | copy-start | bytes 786436
Sparse Core Ops, SparseCore 0:
  22.6 29.7 reduce-scatter.2
  136.2 226.0 reduce-scatter.4
where the time goes:
time: 371 us
  waiting for transfers between devices  248 us (67%)
  blocking collectives  67.9 us (18%)
  matrix products  22 us (6%)
  between operations  14.2 us (4%)
  starting transfers between devices  10.3 us (3%)
  local copies, waits for them, and re-layouts  4.43 us (1%)
    reduce_scatter x1, waiting for transfers between devices, on_device(): lax.psum_scatter(jnp.transpose(product.reshape(tokens, 1 * lax.axis_size(...  210 us
    psum x1, blocking collectives, on_device(): total_squares, total_dots = lax.psum((squares, dot_terms), 'tp')  53.9 us
    reduce_scatter x1, waiting for transfers between devices, on_device(): lax.psum_scatter(jnp.dot(activated, merge_weight, preferred_element_type=...  29 us
    all_to_all x1, blocking collectives, on_device(): lax.all_to_all(returning.reshape(lane_count, slot_count, -1), 'lane', spl...  14 us
    dot_general x1, matrix products, on_device(): jnp.dot(activated, merge_weight, preferred_element_type=jnp.float32)  13.5 us
    all_to_all x1, starting transfers between devices, on_device(): lax.all_to_all(outgoing.reshape(lane_count, slot_count, -1), 'lane', spli...  10.2 us
    all_to_all x1, waiting for transfers between devices, on_device(): lax.all_to_all(outgoing.reshape(lane_count, slot_count, -1), 'lane', spli...  9.52 us
  transfers between devices with their start and end apart: 3, of which 3 were waited for; matrix products, arithmetic and copies ran while one was open for 1% of the time, Pallas kernels for 0%

commit v1 on v0

v1 whole, which is shorter than its diff:
```python
import functools

import jax
import jax.numpy as jnp
from jax import lax
from jax.experimental import pallas as pl
from jax.experimental.pallas import tpu as pltpu
from jax.sharding import PartitionSpec as P

MESH = pl.DeviceIdType.MESH
D = 8192
EPSILON = 1e-06
LANES = 32
TPS = 16
ZS = 8
CAP = 4
SLOTS = LANES * CAP
ROWS = 256
TOKENS = 256
WIDTH = 512
HALF = TOKENS // 2
KV2 = 2048
VD_DEV = 2560
CHUNK = 512
BF16 = jnp.bfloat16
F32 = jnp.float32


def erf(x):
    x = jnp.clip(x, -3.832506856900711, 3.832506856900711)
    y = x * x
    top = 0.00022905065861350646
    for c in (0.0034082910107109506, 0.050955695062380861, 0.18520832239976145, 1.128379143519084):
        top = top * y + c
    low = -1.1791602954361697e-7
    for c in (
        0.000023547966471313185,
        0.0010179625278914885,
        0.014070470171167667,
        0.11098505178285362,
        0.49746925110067538,
        1.0,
    ):
        low = low * y + c
    return x * top / low


def gelu(x):
    return 0.5 * x * (1.0 + erf(x * 0.7071067811865476))


def iota(shape, dim):
    return lax.broadcasted_iota(jnp.int32, shape, dim)


def dot(a, b):
    return jnp.dot(a, b, preferred_element_type=F32)


def dot_t(a, b):
    return lax.dot_general(a, b, (((1,), (1,)), ((), ())), preferred_element_type=F32)


def send_slots(dest):
    lanes = iota((LANES, ROWS), 0)
    matches = lanes == dest
    ones = matches.astype(F32)
    earlier = (iota((ROWS, ROWS), 0) < iota((ROWS, ROWS), 1)).astype(F32)
    before = dot(ones.astype(BF16), earlier.astype(BF16))
    rank = jnp.sum(before * ones, axis=0, keepdims=True).astype(jnp.int32)
    slot = jnp.where(dest >= 0, dest * CAP + rank, -1)
    return (iota((SLOTS, ROWS), 0) == slot).astype(F32)


def to_chunks(rows):
    total = None
    i = iota((SLOTS * 4, SLOTS), 0)
    j = iota((SLOTS * 4, SLOTS), 1)
    for c in range(4):
        pick = (i == (j // 4) * 16 + c * 4 + j % 4).astype(F32).astype(BF16)
        part = dot(pick, rows[:, c * 128 : (c + 1) * 128])
        total = part if total is None else total + part
    return total.astype(BF16).reshape(LANES, 16, 128)


def from_chunks(chunks):
    i = iota((SLOTS, SLOTS * 4), 1)
    j = iota((SLOTS, SLOTS * 4), 0)
    flat = chunks.reshape(SLOTS * 4, 128)
    parts = []
    for c in range(4):
        pick = (i == (j // 4) * 16 + c * 4 + j % 4).astype(F32).astype(BF16)
        parts.append(dot(pick, flat))
    return jnp.concatenate(parts, axis=1).astype(BF16)


def kernel(
    hidden_hbm,
    weight_hbm,
    bias_ref,
    dest_ref,
    pos_ref,
    text_hbm,
    gain_ref,
    kvw_hbm,
    kvg_hbm,
    kv_out,
    embed_out,
    image_out,
    hidden,
    weight,
    text,
    kvw,
    kvg,
    dest_in,
    own_sum,
    part_out,
    part_in,
    grad,
    stream,
    chunk_out,
    chunk_in,
    back_out,
    back_in,
    stat_out,
    stat_in,
    xg,
    prod,
    ring_out,
    ring_in,
    cross_out,
    cross_in,
    load_sem,
    sec_send,
    sec_recv,
    lane_send,
    lane_recv,
    back_send,
    back_recv,
    stat_send,
    stat_recv,
    ring_send,
    ring_recv,
    cross_send,
    cross_recv,
):
    lane = lax.axis_index("lane")
    section = lax.axis_index("section")
    tp = lax.axis_index("tp")
    z = tp // 2
    x_hi = tp % 2
    other = 1 - section

    def load(src, dst, k):
        copy = pltpu.make_async_copy(src, dst, load_sem.at[k])
        copy.start()
        return copy

    load_own = load(hidden_hbm.at[pl.ds(section * ROWS, ROWS)], hidden.at[0], 0)
    load_weight = load(weight_hbm, weight, 1)
    load_other = load(hidden_hbm.at[pl.ds(other * ROWS, ROWS)], hidden.at[1], 2)
    load_kvw = load(kvw_hbm, kvw, 3)
    load_kvg = load(kvg_hbm, kvg, 4)
    load_text = load(text_hbm, text, 5)

    barrier = pltpu.get_barrier_semaphore()

    def greet_lane(p, _):
        pl.semaphore_signal(barrier, inc=1, device_id={"lane": (lane + p) % LANES}, device_id_type=MESH)
        return 0

    def greet_tp(p, _):
        pl.semaphore_signal(barrier, inc=1, device_id={"tp": (tp + p) % TPS}, device_id_type=MESH)
        return 0

    pl.semaphore_signal(barrier, inc=1, device_id={"section": other}, device_id_type=MESH)
    lax.fori_loop(1, LANES, greet_lane, 0)
    lax.fori_loop(1, TPS, greet_tp, 0)

    slots = send_slots(dest_ref[...])
    slots_b = slots.astype(BF16)

    def merge(block, picks):
        total = None
        for k in range(VD_DEV // CHUNK):
            cols = slice(k * CHUNK, (k + 1) * CHUNK)
            picked = dot(picks, hidden[block, :, cols])
            part = dot(gelu(picked).astype(BF16), weight[cols, :])
            total = part if total is None else total + part
        return total

    load_own.wait()
    load_weight.wait()
    own_sum[...] = merge(0, slots_b)

    pl.semaphore_wait(barrier, 1 + (LANES - 1) + (TPS - 1))
    dest_copy = pltpu.make_async_remote_copy(
        dest_ref, dest_in, sec_send.at[0], sec_recv.at[0], device_id={"section": other}, device_id_type=MESH
    )
    dest_copy.start()
    load_kvw.wait()
    load_kvg.wait()
    grad[...] = dot_t(kvg[...], kvw[...])
    dest_copy.wait_recv()
    load_other.wait()
    part_out[...] = merge(1, send_slots(dest_in[...]).astype(BF16)).astype(BF16)
    part_copy = pltpu.make_async_remote_copy(
        part_out, part_in, sec_send.at[1], sec_recv.at[1], device_id={"section": other}, device_id_type=MESH
    )
    part_copy.start()

    place = (iota((TOKENS, SLOTS), 0) == pos_ref[...]).astype(F32)
    is_image = jnp.sum(place, axis=1, keepdims=True) > 0.5
    load_text.wait()

    part_copy.wait_recv()
    image = (own_sum[...] + part_in[...].astype(F32) + bias_ref[...]).astype(BF16)

    def exchange(out_ref, in_ref, send_sem, recv_sem):
        def copy(p):
            peer = (lane + p) % LANES
            return pltpu.make_async_remote_copy(
                out_ref.at[peer],
                in_ref.at[lane],
                send_sem.at[p],
                recv_sem.at[lane],
                device_id={"lane": peer},
                device_id_type=MESH,
            )

        def start(i, _):
            copy(1 + (i + 15) % 31).start()
            return 0

        def wait_recv(p, _):
            peer = (lane + p) % LANES
            pltpu.make_async_remote_copy(
                out_ref.at[peer],
                in_ref.at[peer],
                send_sem.at[p],
                recv_sem.at[peer],
                device_id={"lane": peer},
                device_id_type=MESH,
            ).wait_recv()
            return 0

        def wait_send(p, _):
            copy(p).wait_send()
            return 0

        lax.fori_loop(0, LANES - 1, start, 0)
        in_ref[lane] = out_ref[lane]
        return (
            lambda: lax.fori_loop(1, LANES, wait_recv, 0),
            lambda: lax.fori_loop(1, LANES, wait_send, 0),
        )

    chunk_out[...] = to_chunks(image)
    lane_arrived, lane_sent = exchange(chunk_out, chunk_in, lane_send, lane_recv)
    lane_arrived()

    arrived = from_chunks(chunk_in[...])
    placed = dot(place.astype(BF16), arrived)
    wide = jnp.where(is_image, placed, text[...].astype(F32))
    stream[...] = wide
    gain = gain_ref[...]
    scaled = wide * gain
    squares = jnp.sum(wide * wide, axis=1, keepdims=True)
    dots = jnp.sum(scaled * grad[...], axis=1, keepdims=True)
    first = iota((TOKENS, 128), 1) == 0
    both = jnp.transpose(jnp.where(first, squares, dots))
    stat_out[...] = both[0:2, :]
    stat_in[tp] = both[0:2, :]

    def stat_copy(p, at):
        peer = (tp + p) % TPS
        return pltpu.make_async_remote_copy(
            stat_out,
            stat_in.at[tp if at is None else peer],
            stat_send.at[p],
            stat_recv.at[tp if at is None else peer],
            device_id={"tp": peer},
            device_id_type=MESH,
        )

    def stat_start(p, _):
        stat_copy(p, None).start()
        return 0

    def stat_wait_recv(p, _):
        stat_copy(p, "in").wait_recv()
        return 0

    def stat_wait_send(p, _):
        stat_copy(p, None).wait_send()
        return 0

    lax.fori_loop(1, TPS, stat_start, 0)
    xg[...] = scaled.astype(BF16)

    def project(o):
        block = (z + o) % ZS
        prod[o] = dot(xg[...], kvw[:, pl.ds(pl.multiple_of(block * 256, 256), 256)])

    up = ((z + 1) % ZS) * 2 + x_hi
    down = ((z + ZS - 1) % ZS) * 2 + x_hi
    blocks = ((4, 5, 6, 7), (4, 3, 2, 1), (3, 2, 1), (5, 6, 7))
    targets = (down, up, up, down)
    firsts = (True, False, True, False)

    def rows_of(chain):
        return slice(0, HALF) if firsts[chain] else slice(HALF, TOKENS)

    def ring_copy(chain, step):
        k = chain * 4 + step
        return pltpu.make_async_remote_copy(
            ring_out.at[k],
            ring_in.at[k],
            ring_send.at[k],
            ring_recv.at[k],
            device_id={"tp": targets[chain]},
            device_id_type=MESH,
        )

    ring_copies = []

    def ring_step(chain, step):
        own = prod[blocks[chain][step], rows_of(chain), :]
        if step > 0:
            ring_copy(chain, step - 1).wait_recv()
            own = own + ring_in[chain * 4 + step - 1].astype(F32)
        ring_out[chain * 4 + step] = own.astype(BF16)
        copy = ring_copy(chain, step)
        copy.start()
        ring_copies.append(copy)

    project(4)
    ring_step(0, 0)
    ring_step(1, 0)
    project(3)
    ring_step(2, 0)
    project(5)
    ring_step(3, 0)
    for o in (2, 6, 1, 7, 0):
        project(o)
    for chain in range(4):
        ring_step(chain, 1)

    lax.fori_loop(1, TPS, stat_wait_recv, 0)
    totals = jnp.sum(stat_in[...], axis=0)
    inv_row = lax.rsqrt(totals[0:1, :] / D + EPSILON)
    inv = jnp.transpose(jnp.broadcast_to(inv_row, (128, TOKENS)))
    total_dots = jnp.transpose(jnp.broadcast_to(totals[1:2, :], (128, TOKENS)))
    factor = inv * inv * inv * total_dots / D
    inv4 = jnp.concatenate([inv] * 4, axis=1)
    factor4 = jnp.concatenate([factor] * 4, axis=1)
    embed = (inv4 * gain_ref[...] * grad[...] - stream[...] * factor4).astype(BF16)
    embed_out[...] = embed
    place_t = jnp.transpose(place).astype(BF16)
    back_out[...] = to_chunks(dot(place_t, embed).astype(BF16))
    back_arrived, back_sent = exchange(back_out, back_in, back_send, back_recv)

    for chain in range(4):
        ring_step(chain, 2)
    ring_step(0, 3)
    ring_step(1, 3)

    def ring_end(chain, step):
        ring_copy(chain, step).wait_recv()
        return ring_in[chain * 4 + step].astype(F32)

    first_rows = prod[0, 0:HALF, :] + ring_end(2, 2)
    last_rows = prod[0, HALF:TOKENS, :] + ring_end(3, 2)
    first_rows = first_rows + ring_end(0, 3)
    last_rows = last_rows + ring_end(1, 3)
    summed = jnp.concatenate([first_rows, last_rows], axis=0)
    left, right = summed[:, 0:128], summed[:, 128:256]
    cross_out[...] = jnp.where(x_hi == 0, right, left).astype(BF16)
    kept = jnp.where(x_hi == 0, left, right)
    cross = pltpu.make_async_remote_copy(
        cross_out,
        cross_in,
        cross_send,
        cross_recv,
        device_id={"tp": z * 2 + (1 - x_hi)},
        device_id_type=MESH,
    )
    cross.start()

    back_arrived()
    returned = from_chunks(back_in[...])
    image_out[...] = dot(jnp.transpose(slots).astype(BF16), returned).astype(BF16)

    cross.wait_recv()
    kv_out[...] = (inv * (kept + cross_in[...].astype(F32))).astype(BF16)

    dest_copy.wait_send()
    part_copy.wait_send()
    lane_sent()
    back_sent()
    lax.fori_loop(1, TPS, stat_wait_send, 0)
    for copy in ring_copies:
        copy.wait_send()
    cross.wait_send()


def on_device(
    merge_hidden,
    merge_weight,
    merge_bias,
    row_dest,
    image_pos,
    text_embed,
    norm_gain,
    kv_weight,
    kv_grad,
):
    any_space = pl.BlockSpec(memory_space=pl.ANY)
    vmem = pl.BlockSpec(memory_space=pltpu.VMEM)
    dma = pltpu.SemaphoreType.DMA
    return pl.pallas_call(
        kernel,
        name="step",
        out_shape=(
            jax.ShapeDtypeStruct((TOKENS, KV2 // TPS), BF16),
            jax.ShapeDtypeStruct((TOKENS, WIDTH), BF16),
            jax.ShapeDtypeStruct((ROWS, WIDTH), BF16),
        ),
        in_specs=[any_space, any_space, vmem, vmem, vmem, any_space, vmem, any_space, any_space],
        out_specs=(vmem, vmem, vmem),
        scratch_shapes=[
            pltpu.VMEM((2, ROWS, VD_DEV), BF16),
            pltpu.VMEM((VD_DEV, WIDTH), BF16),
            pltpu.VMEM((TOKENS, WIDTH), BF16),
            pltpu.VMEM((WIDTH, KV2), BF16),
            pltpu.VMEM((TOKENS, KV2), BF16),
            pltpu.VMEM((1, ROWS), jnp.int32),
            pltpu.VMEM((SLOTS, WIDTH), F32),
            pltpu.VMEM((SLOTS, WIDTH), BF16),
            pltpu.VMEM((SLOTS, WIDTH), BF16),
            pltpu.VMEM((TOKENS, WIDTH), F32),
            pltpu.VMEM((TOKENS, WIDTH), F32),
            pltpu.VMEM((LANES, 16, 128), BF16),
            pltpu.VMEM((LANES, 16, 128), BF16),
            pltpu.VMEM((LANES, 16, 128), BF16),
            pltpu.VMEM((LANES, 16, 128), BF16),
            pltpu.VMEM((2, TOKENS), F32),
            pltpu.VMEM((TPS, 2, TOKENS), F32),
            pltpu.VMEM((TOKENS, WIDTH), BF16),
            pltpu.VMEM((ZS, TOKENS, 256), F32),
            pltpu.VMEM((16, HALF, 256), BF16),
            pltpu.VMEM((16, HALF, 256), BF16),
            pltpu.VMEM((TOKENS, 128), BF16),
            pltpu.VMEM((TOKENS, 128), BF16),
            dma((6,)),
            dma((2,)),
            dma((2,)),
            dma((LANES,)),
            dma((LANES,)),
            dma((LANES,)),
            dma((LANES,)),
            dma((TPS,)),
            dma((TPS,)),
            dma((16,)),
            dma((16,)),
            pltpu.SemaphoreType.DMA,
            pltpu.SemaphoreType.DMA,
        ],
        compiler_params=pltpu.CompilerParams(
            collective_id=0, has_side_effects=True, vmem_limit_bytes=60 * 1024 * 1024
        ),
    )(
        merge_hidden,
        merge_weight,
        merge_bias.reshape(1, WIDTH),
        row_dest.reshape(1, ROWS),
        image_pos.reshape(1, SLOTS),
        text_embed,
        norm_gain.reshape(1, WIDTH),
        kv_weight,
        kv_grad,
    )


def solution(mesh):
    in_specs = (
        P("lane", "section"),
        P("section", "tp"),
        P("tp"),
        P(("lane", "section")),
        P("lane", "section", None, None),
        P(("lane", "section"), "tp"),
        P("tp"),
        P("tp", None),
        P(("lane", "section"), None),
    )
    out_specs = (
        P(("lane", "section"), "tp"),
        P(("lane", "section"), "tp"),
        P(("lane", "section"), "tp"),
    )
    return jax.shard_map(on_device, mesh=mesh, in_specs=in_specs, out_specs=out_specs, check_vma=False)
```

time: 371 us -> 70.2 us (0.19)
  waiting for transfers between devices: 248 us -> 0 us
  blocking collectives: 67.9 us -> 0 us
  Pallas kernels: 0 us -> 63.1 us
  matrix products: 22 us -> 0 us
  between operations: 14.2 us -> 0.64 us
  starting transfers between devices: 10.3 us -> 0 us
    reduce_scatter x2 -> x0, waiting for transfers between devices: 239 us -> none  [the longest x1 210 us: on_device(): lax.psum_scatter(jnp.transpose(product.reshape(tokens, 1 * lax.axis_size(...]
    pallas_call x0 -> x1, Pallas kernels: none -> 63.1 us  [on_device(): pl.pallas_call(kernel, name='step', out_shape=(jax.ShapeDtypeStruct((TOKE...]
    psum x1 -> x0, blocking collectives: 53.9 us -> none  [on_device(): total_squares, total_dots = lax.psum((squares, dot_terms), 'tp')]
    dot_general x7 -> x0, matrix products: 22 us -> none  [the longest x1 13.5 us: on_device(): jnp.dot(activated, merge_weight, preferred_element_type=jnp.float32)]
    all_to_all x1 -> x0, blocking collectives: 14 us -> none  [on_device(): lax.all_to_all(returning.reshape(lane_count, slot_count, -1), 'lane', spl...]
    all_to_all x1 -> x0, starting transfers between devices: 10.2 us -> none  [on_device(): lax.all_to_all(outgoing.reshape(lane_count, slot_count, -1), 'lane', spli...]
    all_to_all x1 -> x0, waiting for transfers between devices: 9.52 us -> none  [on_device(): lax.all_to_all(outgoing.reshape(lane_count, slot_count, -1), 'lane', spli...]
    unnamed x15 -> x4, local copies, waits for them, and re-layouts: 1.77 us -> 5.57 us
  transfers between devices with their start and end apart: 3 -> 0, of which waited for: 3 -> 0; matrix products, arithmetic and copies ran while one was open for 1% -> 0% of each run, Pallas kernels for 0% -> 0%
where the time goes in v1:
time: 70.2 us; the launch traced here: 69.9 us
  Pallas kernels  63.1 us (90%)
  local copies, waits for them, and re-layouts  6.19 us (9%)
    pallas_call x1, Pallas kernels, on_device(): pl.pallas_call(kernel, name='step', out_shape=(jax.ShapeDtypeStruct((TOKE...  63.1 us
    unnamed x4, local copies, waits for them, and re-layouts  5.57 us

profile of v1, /device:TPU:16, one launch (start us, length us, event | category | flops | bytes accessed | tf_op | source)
XLA Modules:
  0.0 69.9 jit_solution(8028158566456421633)
XLA Ops:
  0.6 0.8 %copy.13 = s32[1,1,32,4]{3,2,1,0:T(8,128)S(1)} copy(s32[1,1,32,4]{2,3,1,0:T(4,128)} %param.13) | data formatting | bytes 1024 | tf_op args[4]
  1.4 0.6 reshape.20.pos_ref
  2.0 63.1 %step.1 = (bf16[256,128]{1,0:T(8,128)(2,1)}, bf16[256,512]{1,0:T(8,128)(2,1)}, bf16[256,512]{1,0:T(8,128)(2,1)}) custom-call(bf16[512,2560]{1,0:T(8,128)(2,1)} %hidden_hbm.1, bf16[2560,512]{1,0:T(8,128)(2,1)} %weight_hbm.1, f32[1,512]{1,0:T(1,128)} %bitcast.5, s32[1,256]{1,0:T(1,128)} %bitcast.7, s32[1,128]{1,0:T(1,128)} %reshape.20.pos_ref, ...), custom_call_target="tpu_custom_call" | custom-call | tf_op jit(solution)/shard_map/step/pallas_call | solution.py:421
  65.1 1.5 %copy.17 = bf16[256,128]{1,0:T(8,128)(2,1)} copy(bf16[256,128]{1,0:T(8,128)(2,1)} %get-tuple-element.6) | data formatting | bytes 131072
  66.6 1.7 %copy.18 = bf16[256,512]{1,0:T(8,128)(2,1)} copy(bf16[256,512]{1,0:T(8,128)(2,1)} %get-tuple-element.7) | data formatting | bytes 524288
  68.3 1.7 %copy.19 = bf16[256,512]{1,0:T(8,128)(2,1)} copy(bf16[256,512]{1,0:T(8,128)(2,1)} %get-tuple-element.8) | data formatting | bytes 524288

commit v2 on v1

v2 whole, which is shorter than its diff:
```python
import functools

import jax
import jax.numpy as jnp
from jax import lax
from jax.experimental import pallas as pl
from jax.experimental.pallas import tpu as pltpu
from jax.sharding import PartitionSpec as P

MESH = pl.DeviceIdType.MESH
D = 8192
EPSILON = 1e-06
LANES = 32
TPS = 16
ZS = 8
CAP = 4
SLOTS = LANES * CAP
ROWS = 256
TOKENS = 256
WIDTH = 512
HALF = TOKENS // 2
KV2 = 2048
VD_DEV = 2560
CHUNK = 512
BF16 = jnp.bfloat16
F32 = jnp.float32


def erf(x):
    x = jnp.clip(x, -3.832506856900711, 3.832506856900711)
    y = x * x
    top = 0.00022905065861350646
    for c in (0.0034082910107109506, 0.050955695062380861, 0.18520832239976145, 1.128379143519084):
        top = top * y + c
    low = -1.1791602954361697e-7
    for c in (
        0.000023547966471313185,
        0.0010179625278914885,
        0.014070470171167667,
        0.11098505178285362,
        0.49746925110067538,
        1.0,
    ):
        low = low * y + c
    return x * top / low


def gelu(x):
    return 0.5 * x * (1.0 + erf(x * 0.7071067811865476))


def iota(shape, dim):
    return lax.broadcasted_iota(jnp.int32, shape, dim)


def dot(a, b):
    return jnp.dot(a, b, preferred_element_type=F32)


def dot_t(a, b):
    return lax.dot_general(a, b, (((1,), (1,)), ((), ())), preferred_element_type=F32)


def send_slots(dest):
    lanes = iota((LANES, ROWS), 0)
    matches = lanes == dest
    ones = matches.astype(F32)
    earlier = (iota((ROWS, ROWS), 0) < iota((ROWS, ROWS), 1)).astype(F32)
    before = dot(ones.astype(BF16), earlier.astype(BF16))
    rank = jnp.sum(before * ones, axis=0, keepdims=True).astype(jnp.int32)
    slot = jnp.where(dest >= 0, dest * CAP + rank, -1)
    return (iota((SLOTS, ROWS), 0) == slot).astype(F32)


def to_chunks(rows):
    total = None
    i = iota((SLOTS * 4, SLOTS), 0)
    j = iota((SLOTS * 4, SLOTS), 1)
    for c in range(4):
        pick = (i == (j // 4) * 16 + c * 4 + j % 4).astype(F32).astype(BF16)
        part = dot(pick, rows[:, c * 128 : (c + 1) * 128])
        total = part if total is None else total + part
    return total.astype(BF16).reshape(LANES, 16, 128)


def from_chunks(chunks):
    i = iota((SLOTS, SLOTS * 4), 1)
    j = iota((SLOTS, SLOTS * 4), 0)
    flat = chunks.reshape(SLOTS * 4, 128)
    parts = []
    for c in range(4):
        pick = (i == (j // 4) * 16 + c * 4 + j % 4).astype(F32).astype(BF16)
        parts.append(dot(pick, flat))
    return jnp.concatenate(parts, axis=1).astype(BF16)


def kernel(
    hidden_hbm,
    weight_hbm,
    bias_hbm,
    dest_hbm,
    pos_hbm,
    text_hbm,
    gain_hbm,
    kvw_hbm,
    kvg_hbm,
    kv_out,
    embed_out,
    image_out,
    hidden,
    weight,
    bias_ref,
    dest_ref,
    pos_ref,
    text,
    gain_ref,
    kvw,
    kvg,
    own_sum,
    part_out,
    part_in,
    grad,
    stream,
    chunk_out,
    chunk_in,
    back_out,
    back_in,
    stat_out,
    stat_in,
    xg,
    prod,
    ring_out,
    ring_in,
    slot_xg,
    slot_prod,
    slot_out,
    slot_in,
    cross_out,
    cross_in,
    slot_cross_out,
    slot_cross_in,
    load_sem,
    sec_send,
    sec_recv,
    lane_send,
    lane_recv,
    back_send,
    back_recv,
    stat_send,
    stat_recv,
    ring_send,
    ring_recv,
    slot_send,
    slot_recv,
    cross_send,
    cross_recv,
):
    lane = lax.axis_index("lane")
    section = lax.axis_index("section")
    tp = lax.axis_index("tp")
    z = tp // 2
    x_hi = tp % 2
    other = 1 - section

    barrier = pltpu.get_barrier_semaphore()

    def greet_lane(i, _):
        p = 1 + (i + 15) % 31
        pl.semaphore_signal(barrier, inc=1, device_id={"lane": (lane + p) % LANES}, device_id_type=MESH)
        return 0

    def greet_tp(i, _):
        p = 1 + (i + 7) % 15
        pl.semaphore_signal(barrier, inc=1, device_id={"tp": (tp + p) % TPS}, device_id_type=MESH)
        return 0

    def load(src, dst, k):
        copy = pltpu.make_async_copy(src, dst, load_sem.at[k])
        copy.start()
        return copy

    load_dest = load(dest_hbm, dest_ref, 0)
    load_own = load(hidden_hbm.at[pl.ds(section * ROWS, ROWS)], hidden.at[0], 1)
    load_weight = load(weight_hbm, weight, 2)
    lax.fori_loop(0, LANES - 1, greet_lane, 0)
    lax.fori_loop(0, TPS - 1, greet_tp, 0)
    pl.semaphore_signal(barrier, inc=1, device_id={"section": other}, device_id_type=MESH)
    load_other = load(hidden_hbm.at[pl.ds(other * ROWS, ROWS)], hidden.at[1], 3)
    load_pos = load(pos_hbm, pos_ref, 4)
    load_gain = load(gain_hbm, gain_ref, 5)
    load_bias = load(bias_hbm, bias_ref, 6)
    load_text = load(text_hbm, text, 7)
    load_kvw = load(kvw_hbm, kvw, 8)
    load_kvg = load(kvg_hbm, kvg, 9)

    load_dest.wait()
    slots = send_slots(dest_ref[...])
    slots_b = slots.astype(BF16)
    load_own.wait()
    load_weight.wait()
    total = None
    for k in range(VD_DEV // CHUNK):
        cols = slice(k * CHUNK, (k + 1) * CHUNK)
        picked = dot(slots_b, hidden[0, :, cols])
        part = dot(gelu(picked).astype(BF16), weight[cols, :])
        total = part if total is None else total + part
    own_sum[...] = total

    load_other.wait()
    for half in range(2):
        rows = slice(half * HALF, (half + 1) * HALF)
        total = None
        for k in range(VD_DEV // CHUNK):
            cols = slice(k * CHUNK, (k + 1) * CHUNK)
            wide = hidden[1, rows, cols].astype(F32)
            part = dot(gelu(wide).astype(BF16), weight[cols, :])
            total = part if total is None else total + part
        part_out[rows, :] = total.astype(BF16)

    load_pos.wait()
    spread = (iota((LANES, SLOTS), 1) // CAP == iota((LANES, SLOTS), 0)).astype(F32)
    pos_all = dot(pos_ref[...].astype(F32).astype(BF16), spread.astype(BF16))
    pos_own = iota((CAP, SLOTS), 1) % CAP == iota((CAP, SLOTS), 0)
    pos = jnp.sum(jnp.where(pos_own, pos_all, 0.0), axis=0, keepdims=True)
    place = (iota((TOKENS, SLOTS), 0) == pos.astype(jnp.int32)).astype(F32)
    is_image = jnp.sum(place, axis=1, keepdims=True) > 0.5

    load_gain.wait()
    load_bias.wait()
    load_text.wait()
    load_kvw.wait()
    gain = gain_ref[...]
    xg[...] = jnp.where(is_image, 0.0, text[...].astype(F32) * gain).astype(BF16)

    def columns(o):
        block = (z + o) % ZS
        return kvw[:, pl.ds(pl.multiple_of(block * 256, 256), 256)]

    def project(o):
        prod[o] = dot(xg[...], columns(o))

    up = ((z + 1) % ZS) * 2 + x_hi
    down = ((z + ZS - 1) % ZS) * 2 + x_hi
    blocks = ((4, 5, 6, 7), (4, 3, 2, 1), (3, 2, 1), (5, 6, 7))
    targets = (down, up, up, down)
    firsts = (True, False, True, False)

    def ring(out_ref, in_ref, send_sem, recv_sem, prod_ref, half):
        started = []

        def copy_of(chain, step):
            k = chain * 4 + step
            return pltpu.make_async_remote_copy(
                out_ref.at[k],
                in_ref.at[k],
                send_sem.at[k],
                recv_sem.at[k],
                device_id={"tp": targets[chain]},
                device_id_type=MESH,
            )

        def step_of(chain, step):
            rows = slice(0, half) if firsts[chain] else slice(half, 2 * half)
            own = prod_ref[blocks[chain][step], rows, :]
            if step > 0:
                copy_of(chain, step - 1).wait_recv()
                own = own + in_ref[chain * 4 + step - 1].astype(F32)
            out_ref[chain * 4 + step] = own.astype(BF16)
            copy = copy_of(chain, step)
            copy.start()
            started.append(copy)

        def arrived_at(chain, step):
            copy_of(chain, step).wait_recv()
            return in_ref[chain * 4 + step].astype(F32)

        def end():
            first_rows = prod_ref[0, 0:half, :] + arrived_at(2, 2)
            last_rows = prod_ref[0, half : 2 * half, :] + arrived_at(3, 2)
            first_rows = first_rows + arrived_at(0, 3)
            last_rows = last_rows + arrived_at(1, 3)
            summed = jnp.concatenate([first_rows, last_rows], axis=0)
            left, right = summed[:, 0:128], summed[:, 128:256]
            return jnp.where(x_hi == 0, left, right), jnp.where(x_hi == 0, right, left)

        def sent():
            for copy in started:
                copy.wait_send()

        return step_of, end, sent

    text_step, text_end, text_sent = ring(ring_out, ring_in, ring_send, ring_recv, prod, HALF)
    slot_step, slot_end, slot_sent = ring(slot_out, slot_in, slot_send, slot_recv, slot_prod, SLOTS // 2)

    project(4)
    project(3)
    project(5)

    pl.semaphore_wait(barrier, 1 + (LANES - 1) + (TPS - 1))
    part_copy = pltpu.make_async_remote_copy(
        part_out, part_in, sec_send, sec_recv, device_id={"section": other}, device_id_type=MESH
    )
    part_copy.start()
    for chain in range(4):
        text_step(chain, 0)
    for o in (2, 6, 1, 7, 0):
        project(o)
    load_kvg.wait()
    grad[...] = dot_t(kvg[...], kvw[...])

    part_copy.wait_recv()
    image = (own_sum[...] + dot(slots_b, part_in[...]) + bias_ref[...]).astype(BF16)

    def exchange(out_ref, in_ref, send_sem, recv_sem):
        def copy(p):
            peer = (lane + p) % LANES
            return pltpu.make_async_remote_copy(
                out_ref.at[peer],
                in_ref.at[lane],
                send_sem.at[p],
                recv_sem.at[lane],
                device_id={"lane": peer},
                device_id_type=MESH,
            )

        def start(i, _):
            copy(1 + (i + 15) % 31).start()
            return 0

        def wait_recv(p, _):
            peer = (lane + p) % LANES
            pltpu.make_async_remote_copy(
                out_ref.at[peer],
                in_ref.at[peer],
                send_sem.at[p],
                recv_sem.at[peer],
                device_id={"lane": peer},
                device_id_type=MESH,
            ).wait_recv()
            return 0

        def wait_send(p, _):
            copy(p).wait_send()
            return 0

        lax.fori_loop(0, LANES - 1, start, 0)
        in_ref[lane] = out_ref[lane]
        return (
            lambda: lax.fori_loop(1, LANES, wait_recv, 0),
            lambda: lax.fori_loop(1, LANES, wait_send, 0),
        )

    chunk_out[...] = to_chunks(image)
    lane_arrived, lane_sent = exchange(chunk_out, chunk_in, lane_send, lane_recv)

    for chain in range(4):
        text_step(chain, 1)
    for chain in range(4):
        if len(blocks[chain]) > 2:
            text_step(chain, 2)

    lane_arrived()
    arrived = from_chunks(chunk_in[...])
    placed = dot(place.astype(BF16), arrived)
    wide = jnp.where(is_image, placed, text[...].astype(F32))
    stream[...] = wide
    squares = jnp.sum(wide * wide, axis=1, keepdims=True)
    dots = jnp.sum(wide * gain * grad[...], axis=1, keepdims=True)
    first = iota((TOKENS, 128), 1) == 0
    both = jnp.transpose(jnp.where(first, squares, dots))
    stat_out[...] = both[0:2, :]
    stat_in[tp] = both[0:2, :]

    def stat_copy(p, at):
        peer = (tp + p) % TPS
        return pltpu.make_async_remote_copy(
            stat_out,
            stat_in.at[tp if at is None else peer],
            stat_send.at[p],
            stat_recv.at[tp if at is None else peer],
            device_id={"tp": peer},
            device_id_type=MESH,
        )

    def stat_start(i, _):
        stat_copy(1 + (i + 7) % 15, None).start()
        return 0

    def stat_wait_recv(p, _):
        stat_copy(p, "in").wait_recv()
        return 0

    def stat_wait_send(p, _):
        stat_copy(p, None).wait_send()
        return 0

    lax.fori_loop(0, TPS - 1, stat_start, 0)
    slot_xg[...] = (arrived.astype(F32) * gain).astype(BF16)

    def slot_project(o):
        slot_prod[o] = dot(slot_xg[...], columns(o))

    slot_project(4)
    slot_step(0, 0)
    slot_step(1, 0)
    slot_project(3)
    slot_step(2, 0)
    slot_project(5)
    slot_step(3, 0)
    text_step(0, 3)
    text_step(1, 3)
    for o in (2, 6, 1, 7, 0):
        slot_project(o)
    for chain in range(4):
        slot_step(chain, 1)

    def cross_copy(out_ref, in_ref, k):
        return pltpu.make_async_remote_copy(
            out_ref,
            in_ref,
            cross_send.at[k],
            cross_recv.at[k],
            device_id={"tp": z * 2 + (1 - x_hi)},
            device_id_type=MESH,
        )

    text_kept, text_away = text_end()
    cross_out[...] = text_away.astype(BF16)
    text_cross = cross_copy(cross_out, cross_in, 0)
    text_cross.start()

    lax.fori_loop(1, TPS, stat_wait_recv, 0)
    totals = jnp.sum(stat_in[...], axis=0)
    inv_row = lax.rsqrt(totals[0:1, :] / D + EPSILON)
    inv = jnp.transpose(jnp.broadcast_to(inv_row, (128, TOKENS)))
    total_dots = jnp.transpose(jnp.broadcast_to(totals[1:2, :], (128, TOKENS)))
    factor = inv * inv * inv * total_dots / D
    inv4 = jnp.concatenate([inv] * 4, axis=1)
    factor4 = jnp.concatenate([factor] * 4, axis=1)
    embed = (inv4 * gain * grad[...] - stream[...] * factor4).astype(BF16)
    embed_out[...] = embed
    place_t = jnp.transpose(place).astype(BF16)
    back_out[...] = to_chunks(dot(place_t, embed).astype(BF16))
    back_arrived, back_sent = exchange(back_out, back_in, back_send, back_recv)

    for chain in range(4):
        if len(blocks[chain]) > 2:
            slot_step(chain, 2)
    slot_step(0, 3)
    slot_step(1, 3)
    slot_kept, slot_away = slot_end()
    slot_cross_out[...] = slot_away.astype(BF16)
    slot_cross = cross_copy(slot_cross_out, slot_cross_in, 1)
    slot_cross.start()

    back_arrived()
    returned = from_chunks(back_in[...])
    image_out[...] = dot(jnp.transpose(slots).astype(BF16), returned).astype(BF16)

    text_cross.wait_recv()
    text_sum = text_kept + cross_in[...].astype(F32)
    slot_cross.wait_recv()
    slot_sum = slot_kept + slot_cross_in[...].astype(F32)
    high = slot_sum.astype(BF16)
    low = (slot_sum - high.astype(F32)).astype(BF16)
    place_b = place.astype(BF16)
    slot_placed = dot(place_b, high) + dot(place_b, low)
    kv_out[...] = (inv * jnp.where(is_image, slot_placed, text_sum)).astype(BF16)

    part_copy.wait_send()
    lane_sent()
    back_sent()
    lax.fori_loop(1, TPS, stat_wait_send, 0)
    text_sent()
    slot_sent()
    text_cross.wait_send()
    slot_cross.wait_send()


def finish(kv, embed, image, kv_hbm, embed_hbm, image_hbm, sems):
    copies = []
    for k, (src, dst) in enumerate(((embed, embed_hbm), (image, image_hbm), (kv, kv_hbm))):
        copy = pltpu.make_async_copy(src, dst, sems.at[k])
        copy.start()
        copies.append(copy)
    for copy in copies:
        copy.wait()


def on_device(
    merge_hidden,
    merge_weight,
    merge_bias,
    row_dest,
    image_pos,
    text_embed,
    norm_gain,
    kv_weight,
    kv_grad,
):
    any_space = pl.BlockSpec(memory_space=pl.ANY)
    vmem = pl.BlockSpec(memory_space=pltpu.VMEM)
    dma = pltpu.SemaphoreType.DMA
    shapes = ((TOKENS, KV2 // TPS), (TOKENS, WIDTH), (ROWS, WIDTH))
    results = pl.pallas_call(
        kernel,
        name="step",
        out_shape=tuple(pltpu.VMEM(shape, BF16) for shape in shapes),
        in_specs=[any_space] * 9,
        out_specs=(vmem, vmem, vmem),
        scratch_shapes=[
            pltpu.VMEM((2, ROWS, VD_DEV), BF16),
            pltpu.VMEM((VD_DEV, WIDTH), BF16),
            pltpu.VMEM((1, WIDTH), F32),
            pltpu.VMEM((1, ROWS), jnp.int32),
            pltpu.VMEM((CAP, LANES), jnp.int32),
            pltpu.VMEM((TOKENS, WIDTH), BF16),
            pltpu.VMEM((1, WIDTH), F32),
            pltpu.VMEM((WIDTH, KV2), BF16),
            pltpu.VMEM((TOKENS, KV2), BF16),
            pltpu.VMEM((SLOTS, WIDTH), F32),
            pltpu.VMEM((ROWS, WIDTH), BF16),
            pltpu.VMEM((ROWS, WIDTH), BF16),
            pltpu.VMEM((TOKENS, WIDTH), F32),
            pltpu.VMEM((TOKENS, WIDTH), F32),
            pltpu.VMEM((LANES, 16, 128), BF16),
            pltpu.VMEM((LANES, 16, 128), BF16),
            pltpu.VMEM((LANES, 16, 128), BF16),
            pltpu.VMEM((LANES, 16, 128), BF16),
            pltpu.VMEM((2, TOKENS), F32),
            pltpu.VMEM((TPS, 2, TOKENS), F32),
            pltpu.VMEM((TOKENS, WIDTH), BF16),
            pltpu.VMEM((ZS, TOKENS, 256), F32),
            pltpu.VMEM((16, HALF, 256), BF16),
            pltpu.VMEM((16, HALF, 256), BF16),
            pltpu.VMEM((SLOTS, WIDTH), BF16),
            pltpu.VMEM((ZS, SLOTS, 256), F32),
            pltpu.VMEM((16, SLOTS // 2, 256), BF16),
            pltpu.VMEM((16, SLOTS // 2, 256), BF16),
            pltpu.VMEM((TOKENS, 128), BF16),
            pltpu.VMEM((TOKENS, 128), BF16),
            pltpu.VMEM((SLOTS, 128), BF16),
            pltpu.VMEM((SLOTS, 128), BF16),
            dma((10,)),
            pltpu.SemaphoreType.DMA,
            pltpu.SemaphoreType.DMA,
            dma((LANES,)),
            dma((LANES,)),
            dma((LANES,)),
            dma((LANES,)),
            dma((TPS,)),
            dma((TPS,)),
            dma((16,)),
            dma((16,)),
            dma((16,)),
            dma((16,)),
            dma((2,)),
            dma((2,)),
        ],
        compiler_params=pltpu.CompilerParams(
            collective_id=0, has_side_effects=True, vmem_limit_bytes=65011712
        ),
    )(
        merge_hidden,
        merge_weight,
        merge_bias.reshape(1, WIDTH),
        row_dest.reshape(1, ROWS),
        jnp.transpose(image_pos.reshape(LANES, CAP)),
        text_embed,
        norm_gain.reshape(1, WIDTH),
        kv_weight,
        kv_grad,
    )
    return pl.pallas_call(
        finish,
        name="finish",
        out_shape=tuple(jax.ShapeDtypeStruct(shape, BF16) for shape in shapes),
        in_specs=[vmem] * 3,
        out_specs=(any_space,) * 3,
        scratch_shapes=[dma((3,))],
        compiler_params=pltpu.CompilerParams(vmem_limit_bytes=4 * 1024 * 1024),
    )(*results)


def solution(mesh):
    in_specs = (
        P("lane", "section"),
        P("section", "tp"),
        P("tp"),
        P(("lane", "section")),
        P("lane", "section", None, None),
        P(("lane", "section"), "tp"),
        P("tp"),
        P("tp", None),
        P(("lane", "section"), None),
    )
    out_specs = (
        P(("lane", "section"), "tp"),
        P(("lane", "section"), "tp"),
        P(("lane", "section"), "tp"),
    )
    return jax.shard_map(on_device, mesh=mesh, in_specs=in_specs, out_specs=out_specs, check_vma=False)
```

time: 70.2 us -> 61.8 us (0.88)
  local copies, waits for them, and re-layouts: 6.19 us -> 0 us
  Pallas kernels: 63.1 us -> 61 us
    unnamed x4 -> x0, local copies, waits for them, and re-layouts: 5.57 us -> none
    pallas_call x1 -> x2, Pallas kernels: 63.1 us -> 61 us  [the longest x1 60.2 us: on_device(): pl.pallas_call(kernel, name='step', out_shape=tuple((pltpu.VMEM(shape, BF...]
where the time goes in v2:
time: 61.8 us; the launch traced here: 61.7 us
  Pallas kernels  61 us (99%)
  between operations  0.64 us (1%)
    pallas_call x1, Pallas kernels, on_device(): pl.pallas_call(kernel, name='step', out_shape=tuple((pltpu.VMEM(shape, BF...  60.2 us

profile of v2, /device:TPU:16, one launch (start us, length us, event | category | flops | bytes accessed | tf_op | source)
XLA Modules:
  0.0 61.7 jit_solution(12104786350133481921)
XLA Ops:
  0.6 60.2 %step.1 = (bf16[256,128]{1,0:T(8,128)(2,1)S(1)}, bf16[256,512]{1,0:T(8,128)(2,1)S(1)}, bf16[256,512]{1,0:T(8,128)(2,1)S(1)}) custom-call(bf16[512,2560]{1,0:T(8,128)(2,1)} %hidden_hbm.1, bf16[2560,512]{1,0:T(8,128)(2,1)} %weight_hbm.1, f32[1,512]{1,0:T(1,128)} %bitcast.6, s32[1,256]{1,0:T(1,128)} %bitcast.9, s32[4,32]{1,0:T(4,128)} %bitcast.7, ...), custom_call_target="tpu_custom_call" | custom-call | tf_op jit(solution)/shard_map/step/pallas_call | solution.py:505
  60.8 0.8 %finish.1 = (bf16[256,128]{1,0:T(8,128)(2,1)}, bf16[256,512]{1,0:T(8,128)(2,1)}, bf16[256,512]{1,0:T(8,128)(2,1)}) custom-call(bf16[256,128]{1,0:T(8,128)(2,1)S(1)} %get-tuple-element.6.kv, bf16[256,512]{1,0:T(8,128)(2,1)S(1)} %get-tuple-element.7.embed, bf16[256,512]{1,0:T(8,128)(2,1)S(1)} %get-tuple-element.8.image), custom_call_target="tpu_custom_call" | custom-call | tf_op jit(solution)/shard_map/finish/pallas_call | solution.py:574

commit v3 on v2

--- a/solution.py
+++ b/solution.py
@@ -137,8 +137,8 @@
     slot_in,
     cross_out,
     cross_in,
-    slot_cross_out,
-    slot_cross_in,
+    end_out,
+    end_in,
     load_sem,
     sec_send,
     sec_recv,
@@ -152,6 +152,8 @@
     ring_recv,
     slot_send,
     slot_recv,
+    end_send,
+    end_recv,
     cross_send,
     cross_recv,
 ):
@@ -182,8 +184,8 @@
     load_dest = load(dest_hbm, dest_ref, 0)
     load_own = load(hidden_hbm.at[pl.ds(section * ROWS, ROWS)], hidden.at[0], 1)
     load_weight = load(weight_hbm, weight, 2)
-    lax.fori_loop(0, LANES - 1, greet_lane, 0)
-    lax.fori_loop(0, TPS - 1, greet_tp, 0)
+    lax.fori_loop(0, LANES - 1, greet_lane, 0, unroll=True)
+    lax.fori_loop(0, TPS - 1, greet_tp, 0, unroll=True)
     pl.semaphore_signal(barrier, inc=1, device_id={"section": other}, device_id_type=MESH)
     load_other = load(hidden_hbm.at[pl.ds(other * ROWS, ROWS)], hidden.at[1], 3)
     load_pos = load(pos_hbm, pos_ref, 4)
@@ -217,6 +219,11 @@
             total = part if total is None else total + part
         part_out[rows, :] = total.astype(BF16)
 
+    pl.semaphore_wait(barrier, 1 + (LANES - 1) + (TPS - 1))
+    part_copy = pltpu.make_async_remote_copy(
+        part_out, part_in, sec_send, sec_recv, device_id={"section": other}, device_id_type=MESH
+    )
+    part_copy.start()
     load_pos.wait()
     spread = (iota((LANES, SLOTS), 1) // CAP == iota((LANES, SLOTS), 0)).astype(F32)
     pos_all = dot(pos_ref[...].astype(F32).astype(BF16), spread.astype(BF16))
@@ -245,113 +252,94 @@
     targets = (down, up, up, down)
     firsts = (True, False, True, False)
 
-    def ring(out_ref, in_ref, send_sem, recv_sem, prod_ref, half):
-        started = []
-
+    def ring(out_ref, in_ref, send_sem, recv_sem, prod_ref, half, offsets):
         def copy_of(chain, step):
-            k = chain * 4 + step
+            k = offsets[chain] + step
             return pltpu.make_async_remote_copy(
                 out_ref.at[k],
                 in_ref.at[k],
-                send_sem.at[k],
+                send_sem,
                 recv_sem.at[k],
                 device_id={"tp": targets[chain]},
                 device_id_type=MESH,
             )
 
-        def step_of(chain, step):
+        def sum_at(chain, step):
             rows = slice(0, half) if firsts[chain] else slice(half, 2 * half)
             own = prod_ref[blocks[chain][step], rows, :]
             if step > 0:
                 copy_of(chain, step - 1).wait_recv()
-                own = own + in_ref[chain * 4 + step - 1].astype(F32)
-            out_ref[chain * 4 + step] = own.astype(BF16)
-            copy = copy_of(chain, step)
-            copy.start()
-            started.append(copy)
+                own = own + in_ref[offsets[chain] + step - 1].astype(F32)
+            return own
+
+        def step_of(chain, step):
+            out_ref[offsets[chain] + step] = sum_at(chain, step).astype(BF16)
+            copy_of(chain, step).start()
 
         def arrived_at(chain, step):
             copy_of(chain, step).wait_recv()
-            return in_ref[chain * 4 + step].astype(F32)
-
-        def end():
-            first_rows = prod_ref[0, 0:half, :] + arrived_at(2, 2)
-            last_rows = prod_ref[0, half : 2 * half, :] + arrived_at(3, 2)
-            first_rows = first_rows + arrived_at(0, 3)
-            last_rows = last_rows + arrived_at(1, 3)
-            summed = jnp.concatenate([first_rows, last_rows], axis=0)
-            left, right = summed[:, 0:128], summed[:, 128:256]
-            return jnp.where(x_hi == 0, left, right), jnp.where(x_hi == 0, right, left)
-
-        def sent():
-            for copy in started:
-                copy.wait_send()
-
-        return step_of, end, sent
-
-    text_step, text_end, text_sent = ring(ring_out, ring_in, ring_send, ring_recv, prod, HALF)
-    slot_step, slot_end, slot_sent = ring(slot_out, slot_in, slot_send, slot_recv, slot_prod, SLOTS // 2)
+            return in_ref[offsets[chain] + step].astype(F32)
+
+        return step_of, sum_at, arrived_at
+
+    def own_side(block):
+        left, right = block[:, 0:128], block[:, 128:256]
+        return jnp.where(x_hi == 0, left, right), jnp.where(x_hi == 0, right, left)
+
+    text_step, _, text_arrived = ring(ring_out, ring_in, ring_send, ring_recv, prod, HALF, (0, 4, 8, 11))
+    slot_step, slot_at, _ = ring(slot_out, slot_in, slot_send, slot_recv, slot_prod, SLOTS // 2, (0, 3, 6, 8))
+
+    def end_copy(k, count, peer):
+        where = pl.ds(k, count)
+        return pltpu.make_async_remote_copy(
+            end_out.at[where], end_in.at[where], end_send, end_recv, device_id={"tp": peer}, device_id_type=MESH
+        )
+
+    def slot_last(chain):
+        same, away = own_side(slot_at(chain, len(blocks[chain]) - 1))
+        end_out[2 * chain] = same.astype(BF16)
+        end_out[2 * chain + 1] = away.astype(BF16)
+        end_copy(2 * chain, 1, targets[chain]).start()
+        end_copy(2 * chain + 1, 1, targets[chain] + 1 - 2 * x_hi).start()
 
     project(4)
     project(3)
     project(5)
 
-    pl.semaphore_wait(barrier, 1 + (LANES - 1) + (TPS - 1))
-    part_copy = pltpu.make_async_remote_copy(
-        part_out, part_in, sec_send, sec_recv, device_id={"section": other}, device_id_type=MESH
-    )
-    part_copy.start()
     for chain in range(4):
         text_step(chain, 0)
     for o in (2, 6, 1, 7, 0):
         project(o)
+
+    part_copy.wait_recv()
+    image = (own_sum[...] + dot(slots_b, part_in[...]) + bias_ref[...]).astype(BF16)
+
+    def exchange(out_ref, in_ref, send_sem, recv_sem):
+        def start(i, _):
+            peer = (lane + 1 + (i + 15) % 31) % LANES
+            pltpu.make_async_remote_copy(
+                out_ref.at[peer], in_ref.at[lane], send_sem, recv_sem, device_id={"lane": peer}, device_id_type=MESH
+            ).start()
+            return 0
+
+        lax.fori_loop(0, LANES - 1, start, 0, unroll=True)
+        in_ref[lane] = out_ref[lane]
+        every = pl.ds(0, LANES - 1)
+        whole = pltpu.make_async_remote_copy(
+            out_ref.at[every],
+            in_ref.at[every],
+            send_sem,
+            recv_sem,
+            device_id={"lane": (lane + 1) % LANES},
+            device_id_type=MESH,
+        )
+        return whole.wait_recv, whole.wait_send
+
+    chunk_out[...] = to_chunks(image)
+    lane_arrived, lane_sent = exchange(chunk_out, chunk_in, lane_send, lane_recv)
+
     load_kvg.wait()
     grad[...] = dot_t(kvg[...], kvw[...])
-
-    part_copy.wait_recv()
-    image = (own_sum[...] + dot(slots_b, part_in[...]) + bias_ref[...]).astype(BF16)
-
-    def exchange(out_ref, in_ref, send_sem, recv_sem):
-        def copy(p):
-            peer = (lane + p) % LANES
-            return pltpu.make_async_remote_copy(
-                out_ref.at[peer],
-                in_ref.at[lane],
-                send_sem.at[p],
-                recv_sem.at[lane],
-                device_id={"lane": peer},
-                device_id_type=MESH,
-            )
-
-        def start(i, _):
-            copy(1 + (i + 15) % 31).start()
-            return 0
-
-        def wait_recv(p, _):
-            peer = (lane + p) % LANES
-            pltpu.make_async_remote_copy(
-                out_ref.at[peer],
-                in_ref.at[peer],
-                send_sem.at[p],
-                recv_sem.at[peer],
-                device_id={"lane": peer},
-                device_id_type=MESH,
-            ).wait_recv()
-            return 0
-
-        def wait_send(p, _):
-            copy(p).wait_send()
-            return 0
-
-        lax.fori_loop(0, LANES - 1, start, 0)
-        in_ref[lane] = out_ref[lane]
-        return (
-            lambda: lax.fori_loop(1, LANES, wait_recv, 0),
-            lambda: lax.fori_loop(1, LANES, wait_send, 0),
-        )
-
-    chunk_out[...] = to_chunks(image)
-    lane_arrived, lane_sent = exchange(chunk_out, chunk_in, lane_send, lane_recv)
 
     for chain in range(4):
         text_step(chain, 1)
@@ -361,6 +349,18 @@
 
     lane_arrived()
     arrived = from_chunks(chunk_in[...])
+    slot_xg[...] = (arrived.astype(F32) * gain).astype(BF16)
+
+    def slot_project(o):
+        slot_prod[o] = dot(slot_xg[...], columns(o))
+
+    slot_project(4)
+    slot_step(0, 0)
+    slot_step(1, 0)
+    slot_project(3)
+    slot_step(2, 0)
+    slot_project(5)
+    slot_step(3, 0)
     placed = dot(place.astype(BF16), arrived)
     wide = jnp.where(is_image, placed, text[...].astype(F32))
     stream[...] = wide
@@ -371,65 +371,47 @@
     stat_out[...] = both[0:2, :]
     stat_in[tp] = both[0:2, :]
 
-    def stat_copy(p, at):
-        peer = (tp + p) % TPS
-        return pltpu.make_async_remote_copy(
+    def stat_start(i, _):
+        pltpu.make_async_remote_copy(
             stat_out,
-            stat_in.at[tp if at is None else peer],
-            stat_send.at[p],
-            stat_recv.at[tp if at is None else peer],
-            device_id={"tp": peer},
+            stat_in.at[tp],
+            stat_send,
+            stat_recv,
+            device_id={"tp": (tp + 1 + (i + 7) % 15) % TPS},
             device_id_type=MESH,
-        )
-
-    def stat_start(i, _):
-        stat_copy(1 + (i + 7) % 15, None).start()
+        ).start()
         return 0
 
-    def stat_wait_recv(p, _):
-        stat_copy(p, "in").wait_recv()
-        return 0
-
-    def stat_wait_send(p, _):
-        stat_copy(p, None).wait_send()
-        return 0
-
-    lax.fori_loop(0, TPS - 1, stat_start, 0)
-    slot_xg[...] = (arrived.astype(F32) * gain).astype(BF16)
-
-    def slot_project(o):
-        slot_prod[o] = dot(slot_xg[...], columns(o))
-
-    slot_project(4)
-    slot_step(0, 0)
-    slot_step(1, 0)
-    slot_project(3)
-    slot_step(2, 0)
-    slot_project(5)
-    slot_step(3, 0)
+    lax.fori_loop(0, TPS - 1, stat_start, 0, unroll=True)
+
     text_step(0, 3)
     text_step(1, 3)
     for o in (2, 6, 1, 7, 0):
         slot_project(o)
     for chain in range(4):
         slot_step(chain, 1)
-
-    def cross_copy(out_ref, in_ref, k):
-        return pltpu.make_async_remote_copy(
-            out_ref,
-            in_ref,
-            cross_send.at[k],
-            cross_recv.at[k],
-            device_id={"tp": z * 2 + (1 - x_hi)},
-            device_id_type=MESH,
-        )
-
-    text_kept, text_away = text_end()
+    slot_kept, slot_away = own_side(slot_prod[0])
+    end_out[8] = slot_away[0 : SLOTS // 2].astype(BF16)
+    end_out[9] = slot_away[SLOTS // 2 :].astype(BF16)
+    across = z * 2 + (1 - x_hi)
+    end_copy(8, 2, across).start()
+
+    text_first = prod[0, 0:HALF, :] + text_arrived(2, 2)
+    text_last = prod[0, HALF:TOKENS, :] + text_arrived(3, 2)
+    text_first = text_first + text_arrived(0, 3)
+    text_last = text_last + text_arrived(1, 3)
+    text_kept, text_away = own_side(jnp.concatenate([text_first, text_last], axis=0))
     cross_out[...] = text_away.astype(BF16)
-    text_cross = cross_copy(cross_out, cross_in, 0)
+    text_cross = pltpu.make_async_remote_copy(
+        cross_out, cross_in, cross_send, cross_recv, device_id={"tp": across}, device_id_type=MESH
+    )
     text_cross.start()
 
-    lax.fori_loop(1, TPS, stat_wait_recv, 0)
+    each = pl.ds(0, TPS - 1)
+    stat_whole = pltpu.make_async_remote_copy(
+        stat_in.at[each], stat_in.at[each], stat_send, stat_recv, device_id={"tp": across}, device_id_type=MESH
+    )
+    stat_whole.wait_recv()
     totals = jnp.sum(stat_in[...], axis=0)
     inv_row = lax.rsqrt(totals[0:1, :] / D + EPSILON)
     inv = jnp.transpose(jnp.broadcast_to(inv_row, (128, TOKENS)))
@@ -443,15 +425,12 @@
     back_out[...] = to_chunks(dot(place_t, embed).astype(BF16))
     back_arrived, back_sent = exchange(back_out, back_in, back_send, back_recv)
 
-    for chain in range(4):
-        if len(blocks[chain]) > 2:
-            slot_step(chain, 2)
-    slot_step(0, 3)
-    slot_step(1, 3)
-    slot_kept, slot_away = slot_end()
-    slot_cross_out[...] = slot_away.astype(BF16)
-    slot_cross = cross_copy(slot_cross_out, slot_cross_in, 1)
-    slot_cross.start()
+    slot_step(0, 2)
+    slot_step(1, 2)
+    slot_last(2)
+    slot_last(3)
+    slot_last(0)
+    slot_last(1)
 
     back_arrived()
     returned = from_chunks(back_in[...])
@@ -459,8 +438,25 @@
 
     text_cross.wait_recv()
     text_sum = text_kept + cross_in[...].astype(F32)
-    slot_cross.wait_recv()
-    slot_sum = slot_kept + slot_cross_in[...].astype(F32)
+    every_end = pltpu.make_async_remote_copy(
+        end_out, end_in, end_send, end_recv, device_id={"tp": across}, device_id_type=MESH
+    )
+    every_end.wait_recv()
+
+    def ends(up_or_down, own):
+        total = None
+        for k in up_or_down:
+            part = end_in[k].astype(F32)
+            total = part if total is None else total + part
+        return total + own
+
+    slot_sum = jnp.concatenate(
+        [
+            ends((0, 1, 4, 5, 8), slot_kept[0 : SLOTS // 2]),
+            ends((2, 3, 6, 7, 9), slot_kept[SLOTS // 2 :]),
+        ],
+        axis=0,
+    )
     high = slot_sum.astype(BF16)
     low = (slot_sum - high.astype(F32)).astype(BF16)
     place_b = place.astype(BF16)
@@ -470,11 +466,14 @@
     part_copy.wait_send()
     lane_sent()
     back_sent()
-    lax.fori_loop(1, TPS, stat_wait_send, 0)
-    text_sent()
-    slot_sent()
+    stat_whole.wait_send()
+    for out_ref, sem, count in ((ring_out, ring_send, 14), (slot_out, slot_send, 10)):
+        sent = out_ref.at[pl.ds(0, count)]
+        pltpu.make_async_remote_copy(
+            sent, sent, sem, sem, device_id={"tp": across}, device_id_type=MESH
+        ).wait_send()
+    every_end.wait_send()
     text_cross.wait_send()
-    slot_cross.wait_send()
 
 
 def finish(kv, embed, image, kv_hbm, embed_hbm, image_hbm, sems):
@@ -531,31 +530,33 @@
             pltpu.VMEM((TPS, 2, TOKENS), F32),
             pltpu.VMEM((TOKENS, WIDTH), BF16),
             pltpu.VMEM((ZS, TOKENS, 256), F32),
-            pltpu.VMEM((16, HALF, 256), BF16),
-            pltpu.VMEM((16, HALF, 256), BF16),
+            pltpu.VMEM((14, HALF, 256), BF16),
+            pltpu.VMEM((14, HALF, 256), BF16),
             pltpu.VMEM((SLOTS, WIDTH), BF16),
             pltpu.VMEM((ZS, SLOTS, 256), F32),
-            pltpu.VMEM((16, SLOTS // 2, 256), BF16),
-            pltpu.VMEM((16, SLOTS // 2, 256), BF16),
+            pltpu.VMEM((10, SLOTS // 2, 256), BF16),
+            pltpu.VMEM((10, SLOTS // 2, 256), BF16),
             pltpu.VMEM((TOKENS, 128), BF16),
             pltpu.VMEM((TOKENS, 128), BF16),
-            pltpu.VMEM((SLOTS, 128), BF16),
-            pltpu.VMEM((SLOTS, 128), BF16),
+            pltpu.VMEM((10, SLOTS // 2, 128), BF16),
+            pltpu.VMEM((10, SLOTS // 2, 128), BF16),
             dma((10,)),
             pltpu.SemaphoreType.DMA,
             pltpu.SemaphoreType.DMA,
-            dma((LANES,)),
-            dma((LANES,)),
-            dma((LANES,)),
-            dma((LANES,)),
-            dma((TPS,)),
-            dma((TPS,)),
-            dma((16,)),
-            dma((16,)),
-            dma((16,)),
-            dma((16,)),
-            dma((2,)),
-            dma((2,)),
+            pltpu.SemaphoreType.DMA,
+            pltpu.SemaphoreType.DMA,
+            pltpu.SemaphoreType.DMA,
+            pltpu.SemaphoreType.DMA,
+            pltpu.SemaphoreType.DMA,
+            pltpu.SemaphoreType.DMA,
+            pltpu.SemaphoreType.DMA,
+            dma((14,)),
+            pltpu.SemaphoreType.DMA,
+            dma((10,)),
+            pltpu.SemaphoreType.DMA,
+            pltpu.SemaphoreType.DMA,
+            pltpu.SemaphoreType.DMA,
+            pltpu.SemaphoreType.DMA,
         ],
         compiler_params=pltpu.CompilerParams(
             collective_id=0, has_side_effects=True, vmem_limit_bytes=65011712

time: 61.8 us -> 56.6 us (0.916)
  the two profiles are of different devices: /device:TPU:16 before, /device:TPU:14 now
where the time goes in v3:
time: 56.6 us; the launch traced here: 56.5 us
  Pallas kernels  55.9 us (99%)
  between operations  0.64 us (1%)
    pallas_call x1, Pallas kernels, on_device(): pl.pallas_call(kernel, name='step', out_shape=tuple((pltpu.VMEM(shape, BF...  55 us

profile of v3, /device:TPU:14, one launch (start us, length us, event | category | flops | bytes accessed | tf_op | source)
XLA Modules:
  0.0 56.5 jit_solution(6672706328227616065)
XLA Ops:
  0.6 55.0 %step.1 = (bf16[256,128]{1,0:T(8,128)(2,1)S(1)}, bf16[256,512]{1,0:T(8,128)(2,1)S(1)}, bf16[256,512]{1,0:T(8,128)(2,1)S(1)}) custom-call(bf16[512,2560]{1,0:T(8,128)(2,1)} %hidden_hbm.1, bf16[2560,512]{1,0:T(8,128)(2,1)} %weight_hbm.1, f32[1,512]{1,0:T(1,128)} %bitcast.6, s32[1,256]{1,0:T(1,128)} %bitcast.9, s32[4,32]{1,0:T(4,128)} %bitcast.7, ...), custom_call_target="tpu_custom_call" | custom-call | tf_op jit(solution)/shard_map/step/pallas_call | solution.py:504
  55.7 0.8 %finish.1 = (bf16[256,128]{1,0:T(8,128)(2,1)}, bf16[256,512]{1,0:T(8,128)(2,1)}, bf16[256,512]{1,0:T(8,128)(2,1)}) custom-call(bf16[256,128]{1,0:T(8,128)(2,1)S(1)} %get-tuple-element.6.kv, bf16[256,512]{1,0:T(8,128)(2,1)S(1)} %get-tuple-element.7.embed, bf16[256,512]{1,0:T(8,128)(2,1)S(1)} %get-tuple-element.8.image), custom_call_target="tpu_custom_call" | custom-call | tf_op jit(solution)/shard_map/finish/pallas_call | solution.py:575

commit v4 on v3

--- a/solution.py
+++ b/solution.py
@@ -123,6 +123,8 @@
     stream,
     chunk_out,
     chunk_in,
+    image_rows,
+    grad_rows,
     back_out,
     back_in,
     stat_out,
@@ -187,6 +189,11 @@
     lax.fori_loop(0, LANES - 1, greet_lane, 0, unroll=True)
     lax.fori_loop(0, TPS - 1, greet_tp, 0, unroll=True)
     pl.semaphore_signal(barrier, inc=1, device_id={"section": other}, device_id_type=MESH)
+    load_dest.wait()
+    slots = send_slots(dest_ref[...])
+    slots_b = slots.astype(BF16)
+    load_own.wait()
+    load_weight.wait()
     load_other = load(hidden_hbm.at[pl.ds(other * ROWS, ROWS)], hidden.at[1], 3)
     load_pos = load(pos_hbm, pos_ref, 4)
     load_gain = load(gain_hbm, gain_ref, 5)
@@ -194,12 +201,6 @@
     load_text = load(text_hbm, text, 7)
     load_kvw = load(kvw_hbm, kvw, 8)
     load_kvg = load(kvg_hbm, kvg, 9)
-
-    load_dest.wait()
-    slots = send_slots(dest_ref[...])
-    slots_b = slots.astype(BF16)
-    load_own.wait()
-    load_weight.wait()
     total = None
     for k in range(VD_DEV // CHUNK):
         cols = slice(k * CHUNK, (k + 1) * CHUNK)
@@ -313,6 +314,7 @@
 
     part_copy.wait_recv()
     image = (own_sum[...] + dot(slots_b, part_in[...]) + bias_ref[...]).astype(BF16)
+    image_rows[...] = image
 
     def exchange(out_ref, in_ref, send_sem, recv_sem):
         def start(i, _):
@@ -339,7 +341,11 @@
     lane_arrived, lane_sent = exchange(chunk_out, chunk_in, lane_send, lane_recv)
 
     load_kvg.wait()
-    grad[...] = dot_t(kvg[...], kvw[...])
+    normed_grad = dot_t(kvg[...], kvw[...])
+    grad[...] = normed_grad
+    place_t = jnp.transpose(place).astype(BF16)
+    back_out[...] = to_chunks(dot(place_t, normed_grad.astype(BF16)).astype(BF16))
+    back_arrived, back_sent = exchange(back_out, back_in, back_send, back_recv)
 
     for chain in range(4):
         text_step(chain, 1)
@@ -361,6 +367,10 @@
     slot_step(2, 0)
     slot_project(5)
     slot_step(3, 0)
+    text_step(0, 3)
+    text_step(1, 3)
+    for o in (2, 6, 1, 7, 0):
+        slot_project(o)
     placed = dot(place.astype(BF16), arrived)
     wide = jnp.where(is_image, placed, text[...].astype(F32))
     stream[...] = wide
@@ -368,8 +378,16 @@
     dots = jnp.sum(wide * gain * grad[...], axis=1, keepdims=True)
     first = iota((TOKENS, 128), 1) == 0
     both = jnp.transpose(jnp.where(first, squares, dots))
-    stat_out[...] = both[0:2, :]
-    stat_in[tp] = both[0:2, :]
+    stat_out[:, 0:TOKENS] = both[0:2, :]
+
+    back_arrived()
+    grad_rows[...] = from_chunks(back_in[...])
+    rows_wide = image_rows[...].astype(F32)
+    row_squares = jnp.sum(rows_wide * rows_wide, axis=1, keepdims=True)
+    row_dots = jnp.sum(rows_wide * gain * grad_rows[...].astype(F32), axis=1, keepdims=True)
+    row_both = jnp.transpose(jnp.where(iota((SLOTS, 128), 1) == 0, row_squares, row_dots))
+    stat_out[:, TOKENS:] = row_both[0:2, :]
+    stat_in[tp] = stat_out[...]
 
     def stat_start(i, _):
         pltpu.make_async_remote_copy(
@@ -384,10 +402,6 @@
 
     lax.fori_loop(0, TPS - 1, stat_start, 0, unroll=True)
 
-    text_step(0, 3)
-    text_step(1, 3)
-    for o in (2, 6, 1, 7, 0):
-        slot_project(o)
     for chain in range(4):
         slot_step(chain, 1)
     slot_kept, slot_away = own_side(slot_prod[0])
@@ -407,24 +421,6 @@
     )
     text_cross.start()
 
-    each = pl.ds(0, TPS - 1)
-    stat_whole = pltpu.make_async_remote_copy(
-        stat_in.at[each], stat_in.at[each], stat_send, stat_recv, device_id={"tp": across}, device_id_type=MESH
-    )
-    stat_whole.wait_recv()
-    totals = jnp.sum(stat_in[...], axis=0)
-    inv_row = lax.rsqrt(totals[0:1, :] / D + EPSILON)
-    inv = jnp.transpose(jnp.broadcast_to(inv_row, (128, TOKENS)))
-    total_dots = jnp.transpose(jnp.broadcast_to(totals[1:2, :], (128, TOKENS)))
-    factor = inv * inv * inv * total_dots / D
-    inv4 = jnp.concatenate([inv] * 4, axis=1)
-    factor4 = jnp.concatenate([factor] * 4, axis=1)
-    embed = (inv4 * gain * grad[...] - stream[...] * factor4).astype(BF16)
-    embed_out[...] = embed
-    place_t = jnp.transpose(place).astype(BF16)
-    back_out[...] = to_chunks(dot(place_t, embed).astype(BF16))
-    back_arrived, back_sent = exchange(back_out, back_in, back_send, back_recv)
-
     slot_step(0, 2)
     slot_step(1, 2)
     slot_last(2)
@@ -432,9 +428,27 @@
     slot_last(0)
     slot_last(1)
 
-    back_arrived()
-    returned = from_chunks(back_in[...])
-    image_out[...] = dot(jnp.transpose(slots).astype(BF16), returned).astype(BF16)
+    each = pl.ds(0, TPS - 1)
+    stat_whole = pltpu.make_async_remote_copy(
+        stat_in.at[each], stat_in.at[each], stat_send, stat_recv, device_id={"tp": across}, device_id_type=MESH
+    )
+    stat_whole.wait_recv()
+    totals = jnp.sum(stat_in[...], axis=0)
+    inv_row = lax.rsqrt(totals[0:1, :] / D + EPSILON)
+
+    def gradient(where, count, wide, grads):
+        inv = jnp.transpose(jnp.broadcast_to(inv_row[:, where], (128, count)))
+        total_dots = jnp.transpose(jnp.broadcast_to(totals[1:2, where], (128, count)))
+        factor = inv * inv * inv * total_dots / D
+        inv4 = jnp.concatenate([inv] * 4, axis=1)
+        factor4 = jnp.concatenate([factor] * 4, axis=1)
+        return inv, (inv4 * gain * grads - wide * factor4).astype(BF16)
+
+    inv, embed_out[...] = gradient(slice(0, TOKENS), TOKENS, stream[...], grad[...])
+    _, row_grad = gradient(
+        slice(TOKENS, TOKENS + SLOTS), SLOTS, image_rows[...].astype(F32), grad_rows[...].astype(F32)
+    )
+    image_out[...] = dot(jnp.transpose(slots).astype(BF16), row_grad).astype(BF16)
 
     text_cross.wait_recv()
     text_sum = text_kept + cross_in[...].astype(F32)
@@ -524,10 +538,12 @@
             pltpu.VMEM((TOKENS, WIDTH), F32),
             pltpu.VMEM((LANES, 16, 128), BF16),
             pltpu.VMEM((LANES, 16, 128), BF16),
+            pltpu.VMEM((SLOTS, WIDTH), BF16),
+            pltpu.VMEM((SLOTS, WIDTH), BF16),
             pltpu.VMEM((LANES, 16, 128), BF16),
             pltpu.VMEM((LANES, 16, 128), BF16),
-            pltpu.VMEM((2, TOKENS), F32),
-            pltpu.VMEM((TPS, 2, TOKENS), F32),
+            pltpu.VMEM((2, TOKENS + SLOTS), F32),
+            pltpu.VMEM((TPS, 2, TOKENS + SLOTS), F32),
             pltpu.VMEM((TOKENS, WIDTH), BF16),
             pltpu.VMEM((ZS, TOKENS, 256), F32),
             pltpu.VMEM((14, HALF, 256), BF16),

time: 56.6 us -> 55.5 us (0.981)
  the two profiles are of different devices: /device:TPU:14 before, /device:TPU:2 now
where the time goes in v4:
time: 55.5 us; the launch traced here: 55.4 us
  Pallas kernels  54.7 us (99%)
  between operations  0.64 us (1%)
    pallas_call x1, Pallas kernels, on_device(): pl.pallas_call(kernel, name='step', out_shape=tuple((pltpu.VMEM(shape, BF...  53.9 us

profile of v4, /device:TPU:2, one launch (start us, length us, event | category | flops | bytes accessed | tf_op | source)
XLA Modules:
  0.0 55.4 jit_solution(10198192538059593033)
XLA Ops:
  0.6 53.9 %step.1 = (bf16[256,128]{1,0:T(8,128)(2,1)S(1)}, bf16[256,512]{1,0:T(8,128)(2,1)S(1)}, bf16[256,512]{1,0:T(8,128)(2,1)S(1)}) custom-call(bf16[512,2560]{1,0:T(8,128)(2,1)} %hidden_hbm.1, bf16[2560,512]{1,0:T(8,128)(2,1)} %weight_hbm.1, f32[1,512]{1,0:T(1,128)} %bitcast.6, s32[1,256]{1,0:T(1,128)} %bitcast.9, s32[4,32]{1,0:T(4,128)} %bitcast.7, ...), custom_call_target="tpu_custom_call" | custom-call | tf_op jit(solution)/shard_map/step/pallas_call | solution.py:518
  54.5 0.8 %finish.1 = (bf16[256,128]{1,0:T(8,128)(2,1)}, bf16[256,512]{1,0:T(8,128)(2,1)}, bf16[256,512]{1,0:T(8,128)(2,1)}) custom-call(bf16[256,128]{1,0:T(8,128)(2,1)S(1)} %get-tuple-element.6.kv, bf16[256,512]{1,0:T(8,128)(2,1)S(1)} %get-tuple-element.7.embed, bf16[256,512]{1,0:T(8,128)(2,1)S(1)} %get-tuple-element.8.image), custom_call_target="tpu_custom_call" | custom-call | tf_op jit(solution)/shard_map/finish/pallas_call | solution.py:591

commit v5 on v4

--- a/solution.py
+++ b/solution.py
@@ -371,6 +371,8 @@
     text_step(1, 3)
     for o in (2, 6, 1, 7, 0):
         slot_project(o)
+    for chain in range(4):
+        slot_step(chain, 1)
     placed = dot(place.astype(BF16), arrived)
     wide = jnp.where(is_image, placed, text[...].astype(F32))
     stream[...] = wide
@@ -402,8 +404,6 @@
 
     lax.fori_loop(0, TPS - 1, stat_start, 0, unroll=True)
 
-    for chain in range(4):
-        slot_step(chain, 1)
     slot_kept, slot_away = own_side(slot_prod[0])
     end_out[8] = slot_away[0 : SLOTS // 2].astype(BF16)
     end_out[9] = slot_away[SLOTS // 2 :].astype(BF16)

time: 55.5 us -> 55 us (level)
  no operation moved by 1% of the time
where the time goes in v5:
time: 55 us; the launch traced here: 54.8 us
  Pallas kernels  54.2 us (99%)
  between operations  0.64 us (1%)
    pallas_call x1, Pallas kernels, on_device(): pl.pallas_call(kernel, name='step', out_shape=tuple((pltpu.VMEM(shape, BF...  53.4 us

profile of v5, /device:TPU:2, one launch (start us, length us, event | category | flops | bytes accessed | tf_op | source)
XLA Modules:
  0.0 54.8 jit_solution(7030159188230292351)
XLA Ops:
  0.6 53.4 %step.1 = (bf16[256,128]{1,0:T(8,128)(2,1)S(1)}, bf16[256,512]{1,0:T(8,128)(2,1)S(1)}, bf16[256,512]{1,0:T(8,128)(2,1)S(1)}) custom-call(bf16[512,2560]{1,0:T(8,128)(2,1)} %hidden_hbm.1, bf16[2560,512]{1,0:T(8,128)(2,1)} %weight_hbm.1, f32[1,512]{1,0:T(1,128)} %bitcast.6, s32[1,256]{1,0:T(1,128)} %bitcast.9, s32[4,32]{1,0:T(4,128)} %bitcast.7, ...), custom_call_target="tpu_custom_call" | custom-call | tf_op jit(solution)/shard_map/step/pallas_call | solution.py:518
  54.0 0.8 %finish.1 = (bf16[256,128]{1,0:T(8,128)(2,1)}, bf16[256,512]{1,0:T(8,128)(2,1)}, bf16[256,512]{1,0:T(8,128)(2,1)}) custom-call(bf16[256,128]{1,0:T(8,128)(2,1)S(1)} %get-tuple-element.6.kv, bf16[256,512]{1,0:T(8,128)(2,1)S(1)} %get-tuple-element.7.embed, bf16[256,512]{1,0:T(8,128)(2,1)S(1)} %get-tuple-element.8.image), custom_call_target="tpu_custom_call" | custom-call | tf_op jit(solution)/shard_map/finish/pallas_call | solution.py:591
